TPU v7x, 512 devices: a whole 4x4x16 slice. The times are simulated.
512 devices in a mesh: dp: 128 (over z, x, core), mp: 4 (over y).
Axes of the slice: x: 4, y: 4, z: 16, core: 2. Of those that a mesh axis runs over, the one named last changes fastest.
Arguments:
- session_length: int32 [128], P('dp'), may hold values from 1 to 128
- event_owner: int32 [16384, 1], P('dp'), may hold values from 0 to 127; in each aligned block of 128 rows (0 to 127, 128 to 255, ...) at most 2 rows name the same one
- event_row: int32 [16384], P('dp'), may hold values from 0 to 255
- text_rows: bfloat16 [32768, 4096], P('dp', 'mp'), may hold values from -6 to 6
- image_rows: bfloat16 [32768, 4096], P('dp', 'mp'), may hold values from -6 to 6
- price: float32 [32768], P('dp'), may hold values from 0.2 to 5
- price_dir: bfloat16 [4096], P('mp'), may hold values from -4 to 4
- norm_gain: bfloat16 [4096], P('mp'), may hold values from 0.5 to 1.5
- w_query: bfloat16 [4096, 2048], P('dp', 'mp'), may hold values from -1 to 1
- w_key: bfloat16 [4096, 2048], P('dp', 'mp'), may hold values from -1 to 1
- w_value: bfloat16 [4096, 2048], P('dp', 'mp'), may hold values from -0.09375 to 0.09375
- cotangent: bfloat16 [16384, 4096], P('dp', 'mp'), may hold values from -6 to 6
Outputs:
- context: bfloat16 [16384, 2048], P('dp', 'mp')
- text_grad: float32 [32768, 4096], P('dp', 'mp')
- image_grad: float32 [32768, 4096], P('dp', 'mp')
Inputs may be any that keep to these rules, and one draw needn't show every extreme that they name: `event_owner`: among the event slots of one index of dp, no owner is named more than 2 times, a bound that some block reaches.
All inputs are finite; a program needn't handle non-finite values.
Results may differ from a plain program's by a relative error of at most 0.0063.
Values may be sent and summed in bfloat16 or wider, within the bound.
No kernel may reach another device: no remote copies, remote signals or barrier semaphores. Data moves between devices by JAX's collectives and lax.ppermute only.
A program may use at most 64 MiB of HBM per device.

v0:
```python
import math
import jax
import jax.numpy as jnp
from jax import lax
from jax.sharding import PartitionSpec as P

D = 4096
HD = 128
SLOT = 128


def fetch_rows(requests, text_rows, image_rows):
    row_ids = jnp.maximum(requests, 0)
    return (row_ids, text_rows[row_ids], image_rows[row_ids])


def join_rows(row_ids, text_got, image_got, price, price_dir):
    price_got = price[row_ids]
    mixed = text_got.astype(jnp.float32) * image_got.astype(jnp.float32) + price_got[
        ..., None
    ] * price_dir.astype(jnp.float32)
    return mixed.astype(jnp.bfloat16)


def answer(requests, text_rows, image_rows, price, price_dir):
    row_ids, text_got, image_got = fetch_rows(requests, text_rows, image_rows)
    joined_rows = join_rows(row_ids, text_got, image_got, price, price_dir)
    replies = lax.all_to_all(joined_rows, "dp", split_axis=0, concat_axis=0, tiled=True)
    return (replies, row_ids, text_got, image_got)


def credit_rows(row_ids, grad_rows, text_got, image_got, table_rows):
    col_width = grad_rows.shape[-1]
    flat_ids = row_ids.reshape(-1)
    grad_float = grad_rows.astype(jnp.float32)
    text_terms = (grad_float * image_got.astype(jnp.float32)).reshape(-1, col_width)
    image_terms = (grad_float * text_got.astype(jnp.float32)).reshape(-1, col_width)
    text_grad = jax.ops.segment_sum(text_terms, flat_ids, num_segments=table_rows)
    image_grad = jax.ops.segment_sum(image_terms, flat_ids, num_segments=table_rows)
    return (text_grad, image_grad)


def attend(query, keys, values, session_length):
    sessions = session_length.shape[0]
    heads_here = query.shape[1] // HD
    shape4 = (sessions, SLOT, heads_here, HD)
    scores = jnp.einsum(
        "sqhd,skhd->shqk",
        query.reshape(shape4),
        keys.reshape(shape4),
        preferred_element_type=jnp.float32,
    ) / math.sqrt(HD)
    position = jnp.arange(SLOT, dtype=jnp.int32)
    live_mask = position[None, :] < session_length[:, None]
    allowed = (position[None, :] <= position[:, None])[None, None, :, :] & live_mask[
        :, None, None, :
    ]
    scores = jnp.where(allowed, scores, jnp.float32(-1e30))
    row_max = jnp.max(scores, axis=-1, keepdims=True)
    powers = jnp.exp(scores - row_max)
    probs = (powers / jnp.sum(powers, axis=-1, keepdims=True)).astype(jnp.bfloat16)
    context = jnp.einsum(
        "shqk,skhd->sqhd", probs, values.reshape(shape4), preferred_element_type=jnp.float32
    )
    context = jnp.where(live_mask[:, :, None, None], context, jnp.float32(0.0))
    return context.reshape(sessions * SLOT, heads_here * HD).astype(jnp.bfloat16)


def local(
    session_length,
    event_owner,
    event_row,
    text_rows,
    image_rows,
    price,
    price_dir,
    norm_gain,
    w_query,
    w_key,
    w_value,
    cotangent,
):
    peers = lax.axis_size("dp")
    tok_count = event_row.shape[0]
    capacity = 2 * tok_count // peers
    col_width = text_rows.shape[1]
    table_rows = text_rows.shape[0]
    owner_ids = event_owner[:, 0]
    member = (owner_ids[:, None] == jnp.arange(peers, dtype=jnp.int32)[None, :]).astype(jnp.int32)
    earlier = jnp.sum((jnp.cumsum(member, axis=0) - member) * member, axis=1)
    slot_ids = owner_ids * capacity + earlier
    requests = (
        jnp.full((peers * capacity,), -1, jnp.int32)
        .at[slot_ids]
        .set(event_row)
        .reshape(peers, capacity)
    )
    grad_buffer = (
        jnp.zeros((peers * capacity, col_width), jnp.bfloat16)
        .at[slot_ids]
        .set(cotangent)
        .reshape(peers, capacity, col_width)
    )
    replies = answer(
        lax.all_to_all(requests, "dp", split_axis=0, concat_axis=0, tiled=True),
        text_rows,
        image_rows,
        price,
        price_dir,
    )[0]
    got_ids, got_grads = (
        lax.all_to_all(requests, "dp", split_axis=0, concat_axis=0, tiled=True),
        lax.all_to_all(grad_buffer, "dp", split_axis=0, concat_axis=0, tiled=True),
    )
    row_ids, text_got, image_got = fetch_rows(got_ids, text_rows, image_rows)
    text_grad, image_grad = credit_rows(row_ids, got_grads, text_got, image_got, table_rows)
    joined_rows = replies.reshape(peers * capacity, col_width)[slot_ids]
    joined_float = joined_rows.astype(jnp.float32)
    square_sums = lax.psum(jnp.sum(joined_float * joined_float, axis=1), "mp")
    scale = lax.rsqrt(square_sums / D + 1e-06)
    normed = (joined_float * scale[:, None] * norm_gain.astype(jnp.float32)[None, :]).astype(
        jnp.bfloat16
    )
    features_all = lax.all_gather(normed, "mp", axis=1, tiled=True)

    def add_rows(weight_rows):
        return jnp.dot(features_all, weight_rows, preferred_element_type=jnp.float32)

    query_sum = add_rows(lax.all_gather(w_query, "dp", axis=0, tiled=True))
    key_sum = add_rows(lax.all_gather(w_key, "dp", axis=0, tiled=True))
    value_sum = add_rows(lax.all_gather(w_value, "dp", axis=0, tiled=True))
    context = attend(
        query_sum.astype(jnp.bfloat16),
        key_sum.astype(jnp.bfloat16),
        value_sum.astype(jnp.bfloat16),
        session_length,
    )
    return (context, text_grad, image_grad)


def solution(mesh):
    return jax.shard_map(
        local,
        mesh=mesh,
        in_specs=(
            P("dp"),
            P("dp", None),
            P("dp"),
            P("dp", "mp"),
            P("dp", "mp"),
            P("dp"),
            P("mp"),
            P("mp"),
            P("dp", "mp"),
            P("dp", "mp"),
            P("dp", "mp"),
            P("dp", "mp"),
        ),
        out_specs=(P("dp", "mp"), P("dp", "mp"), P("dp", "mp")),
        check_vma=False,
    )
```

profile of v0, /device:TPU:1, one launch (start us, length us, event | category | flops | bytes accessed | tf_op | source)
XLA Modules:
  0.0 602.6 jit_solution(7912905382597587258)
XLA Ops:
  7.2 0.0 copy-start
  7.2 0.8 fusion.22
  8.0 0.2 reduce_window_sum.11
  8.2 0.8 select_reduce_fusion
  9.0 0.7 fusion.24
  9.7 1.1 scatter_custom_fusion
  10.8 0.8 all_to_all.13
  11.5 20.4 %all-to-all-start = ((s32[128,1,2]{2,1,0:T(1,128)}), s32[128,1,2]{2,1,0:T(1,128)S(1)}, u32[]{:S(2)}, u32[]{:S(2)}) async-start(s32[128,1,2]{2,1,0:T(1,128)} %bitcast.4), calls=%async_computation | async-start | bytes 131072 | tf_op jit(solution)/shard_map/all_to_all | solution.py:105
  31.9 1.7 scatter_custom_fusion.1
  33.7 0.0 copy-start.1
  33.7 1.0 reshape.139
  34.7 12.1 %all-to-all-done = s32[128,1,2]{2,1,0:T(1,128)S(1)} async-done(((s32[128,1,2]{2,1,0:T(1,128)}), s32[128,1,2]{2,1,0:T(1,128)S(1)}, u32[]{:S(2)}, u32[]{:S(2)}) %all-to-all-start) | async-done | bytes 1056 | tf_op jit(solution)/shard_map/all_to_all | solution.py:105
  46.8 5.7 all-to-all-start.2
  52.4 0.7 convert_element_type.54
  53.1 0.2 maximum_reduce_fusion
  53.3 0.1 reshape.144
  53.5 0.0 copy-done
  53.5 1.2 gather_fusion
  54.7 1.6 reshape.214
  56.3 0.0 copy-done.1
  56.3 0.0 copy-start.2
  56.3 1.9 gather_fusion.2
  58.2 0.1 reshape.159
  58.4 0.0 copy-done.2
  58.4 1.2 gather_fusion.1
  59.6 0.0 copy-start.4
  59.6 1.6 reshape.215
  61.2 22.5 %all-to-all-done.2 = bf16[128,2,1024]{2,1,0:T(2,128)(2,1)S(1)} async-done(((bf16[128,2,1024]{2,1,0:T(2,128)(2,1)}), bf16[128,2,1024]{2,1,0:T(2,128)(2,1)S(1)}, u32[]{:S(2)}, u32[]{:S(2)}) %all-to-all-start.2) | async-done | bytes 524320 | tf_op jit(solution)/shard_map/all_to_all | solution.py:113
  83.7 3.1 convert_multiply_fusion
  86.9 9.2 %all-to-all-start.1 = ((bf16[128,2,1024]{2,1,0:T(2,128)(2,1)}), bf16[128,2,1024]{2,1,0:T(2,128)(2,1)}, u32[]{:S(2)}, u32[]{:S(2)}) async-start(bf16[128,2,1024]{2,1,0:T(2,128)(2,1)} %get-tuple-element.13), calls=%async_computation.1 | async-start | bytes 1048576 | tf_op jit(solution)/shard_map/all_to_all | solution.py:28
  96.1 0.2 all-gather.5.cloned.1.call-start
  96.3 0.0 copy-done.4
  96.4 30.2 %all-to-all-done.1 = bf16[128,2,1024]{2,1,0:T(2,128)(2,1)} async-done(((bf16[128,2,1024]{2,1,0:T(2,128)(2,1)}), bf16[128,2,1024]{2,1,0:T(2,128)(2,1)}, u32[]{:S(2)}, u32[]{:S(2)}) %all-to-all-start.1) | async-done | bytes 524320 | tf_op jit(solution)/shard_map/all_to_all | solution.py:28
  126.6 1.2 reshape.135
  127.8 0.9 gather_fusion.3
  128.7 0.1 fusion.8
  128.8 8.7 %psum.7 = f32[128]{0:T(128)S(1)} all-reduce(f32[128]{0:T(128)S(1)} %fusion.8), channel_id=1, replica_groups=mesh['dp'=128,'mp'=4] {'mp'}, use_global_device_ids=true, to_apply=%region_4.5 | all-reduce | flops 128 | bytes 1024 | tf_op jit(solution)/shard_map/psum | solution.py:119
  137.6 0.8 fusion.10
  138.4 0.0 all-gather.5.cloned.1.call-update
  138.4 0.0 all-gather.7.cloned.1.call-start
  138.5 0.7 all-gather.7.cloned.1.call-update
  139.2 0.0 all-gather.11.cloned.1.call-start
  139.2 0.7 all-gather.11.cloned.1.call-update
  139.9 0.0 all-gather.9.cloned.1.call-start
  139.9 0.5 all-gather.9.cloned.1.call-update
  141.1 0.1 fusion.23
  141.2 1.7 reshape.194
  142.9 0.7 reshape.202
  143.6 4.3 scatter_custom_fusion.2
  147.9 3.6 scatter_custom_fusion.3
  151.5 11.5 %all-gather.5.cloned.1.call-done = bf16[128,4096]{1,0:T(8,128)(2,1)} async-done(((bf16[128,1024]{1,0:T(8,128)(2,1)}), bf16[128,4096]{1,0:T(8,128)(2,1)}) %all-gather.5.cloned.1.call-update) | async-done | bytes 1048592 | tf_op jit(solution)/shard_map/all_gather | solution.py:124
  163.0 0.0 copy-start.3
  163.0 146.8 %all-gather.7.cloned.1.call-done = bf16[4096,512]{1,0:T(8,128)(2,1)} async-done(((bf16[32,512]{1,0:T(8,128)(2,1)}), bf16[4096,512]{1,0:T(8,128)(2,1)}) %all-gather.7.cloned.1.call-update) | async-done | bytes 4194320 | tf_op jit(solution)/shard_map/all_gather | solution.py:131
  309.8 3.2 convolution_convert_fusion.2
  313.1 0.1 copy.32
  313.2 137.7 %all-gather.11.cloned.1.call-done = bf16[4096,512]{1,0:T(8,128)(2,1)} async-done(((bf16[32,512]{1,0:T(8,128)(2,1)}), bf16[4096,512]{1,0:T(8,128)(2,1)}) %all-gather.11.cloned.1.call-update) | async-done | bytes 4194320 | tf_op jit(solution)/shard_map/all_gather | solution.py:130
  450.9 0.0 copy-done.3
  450.9 2.9 fusion.7
  453.8 138.0 %all-gather.9.cloned.1.call-done = bf16[4096,512]{1,0:T(8,128)(2,1)} async-done(((bf16[32,512]{1,0:T(8,128)(2,1)}), bf16[4096,512]{1,0:T(8,128)(2,1)}) %all-gather.9.cloned.1.call-update) | async-done | bytes 4194320 | tf_op jit(solution)/shard_map/all_gather | solution.py:129
  591.9 2.9 fusion.6
  594.8 0.2 fusion.2
  595.0 0.1 fusion.28
  595.1 0.2 fusion.5
  595.3 0.8 copy.30
  (5 shorter events, 0.0 us)
Async XLA Ops:
  7.2 46.3 %copy-start = (bf16[256,1024]{1,0:T(8,128)(2,1)S(1)}, bf16[256,1024]{1,0:T(8,128)(2,1)}, u32[]{:S(2)}) copy-start(bf16[256,1024]{1,0:T(8,128)(2,1)} %param.15) | copy-start | bytes 1572868
  11.5 35.2 %all-to-all-start = ((s32[128,1,2]{2,1,0:T(1,128)}), s32[128,1,2]{2,1,0:T(1,128)S(1)}, u32[]{:S(2)}, u32[]{:S(2)}) async-start(s32[128,1,2]{2,1,0:T(1,128)} %bitcast.4), calls=%async_computation | async-start | bytes 131072 | tf_op jit(solution)/shard_map/all_to_all | solution.py:105
  33.7 22.6 %copy-start.1 = (f32[256]{0:T(256)S(1)}, f32[256]{0:T(256)}, u32[]{:S(2)}) copy-start(f32[256]{0:T(256)} %param.17) | copy-start | bytes 3076
  46.8 37.0 %all-to-all-start.2 = ((bf16[128,2,1024]{2,1,0:T(2,128)(2,1)}), bf16[128,2,1024]{2,1,0:T(2,128)(2,1)S(1)}, u32[]{:S(2)}, u32[]{:S(2)}) async-start(bf16[128,2,1024]{2,1,0:T(2,128)(2,1)} %reshape.139), calls=%async_computation.2 | async-start | bytes 1048576 | tf_op jit(solution)/shard_map/all_to_all | solution.py:113
  56.3 2.1 copy-start.2
  59.6 36.8 %copy-start.4 = (bf16[1024]{0:T(1024)(128)(2,1)S(1)}, bf16[1024]{0:T(1024)(128)(2,1)}, u32[]{:S(2)}) copy-start(bf16[1024]{0:T(1024)(128)(2,1)} %param.19) | copy-start | bytes 6148
  86.9 39.7 %all-to-all-start.1 = ((bf16[128,2,1024]{2,1,0:T(2,128)(2,1)}), bf16[128,2,1024]{2,1,0:T(2,128)(2,1)}, u32[]{:S(2)}, u32[]{:S(2)}) async-start(bf16[128,2,1024]{2,1,0:T(2,128)(2,1)} %get-tuple-element.13), calls=%async_computation.1 | async-start | bytes 1048576 | tf_op jit(solution)/shard_map/all_to_all | solution.py:28
  96.1 66.9 %all-gather.5.cloned.1.call-start = ((), (), s32[]{:S(2)}) async-start(), calls=%async_computation.3 | async-start | bytes 1310720 | tf_op jit(solution)/shard_map/all_gather | solution.py:124
  138.4 171.4 %all-gather.7.cloned.1.call-start = ((), (), s32[]{:S(2)}) async-start(), calls=%async_computation.4 | async-start | bytes 4227072 | tf_op jit(solution)/shard_map/all_gather | solution.py:131
  139.2 311.8 %all-gather.11.cloned.1.call-start = ((), (), s32[]{:S(2)}) async-start(), calls=%async_computation.6 | async-start | bytes 4227072 | tf_op jit(solution)/shard_map/all_gather | solution.py:130
  139.9 452.0 %all-gather.9.cloned.1.call-start = ((), (), s32[]{:S(2)}) async-start(), calls=%async_computation.5 | async-start | bytes 4227072 | tf_op jit(solution)/shard_map/all_gather | solution.py:129
  163.0 287.9 %copy-start.3 = (bf16[128,4096]{1,0:T(8,128)(2,1)S(1)}, bf16[128,4096]{1,0:T(8,128)(2,1)}, u32[]{:S(2)}) copy-start(bf16[128,4096]{1,0:T(8,128)(2,1)} %all-gather.5.cloned.1.call-done) | copy-start | bytes 3145732
Sparse Core Ops, SparseCore 0:
  138.5 24.4 all-gather.4
  166.2 143.6 all-gather.6
  313.0 137.8 all-gather.10
  453.9 137.9 all-gather.8
where the time goes:
time: 603 us
  waiting for transfers between devices  501 us (83%)
  starting transfers between devices  35.6 us (6%)
  local copies, waits for them, and re-layouts  17.8 us (3%)
  other arithmetic  15.6 us (3%)
  between operations  14.6 us (2%)
  matrix products  9.46 us (2%)
  blocking collectives  8.72 us (1%)
    all_gather x1, waiting for transfers between devices, local(): value_sum = add_rows(lax.all_gather(w_value, 'dp', axis=0, tiled=True))  147 us
    all_gather x1, waiting for transfers between devices, local(): query_sum = add_rows(lax.all_gather(w_query, 'dp', axis=0, tiled=True))  138 us
    all_gather x1, waiting for transfers between devices, local(): key_sum = add_rows(lax.all_gather(w_key, 'dp', axis=0, tiled=True))  138 us
    all_to_all x1, waiting for transfers between devices, answer(): lax.all_to_all(joined_rows, 'dp', split_axis=0, concat_axis=0, tiled=True)  30.2 us
    all_to_all x1, waiting for transfers between devices, local(): lax.all_to_all(grad_buffer, 'dp', split_axis=0, concat_axis=0, tiled=True)  22.5 us
    all_to_all x1, starting transfers between devices, local(): lax.all_to_all(requests, 'dp', split_axis=0, concat_axis=0, tiled=True)  20.4 us
    all_to_all x1, waiting for transfers between devices, local(): lax.all_to_all(requests, 'dp', split_axis=0, concat_axis=0, tiled=True)  12.1 us
  transfers between devices with their start and end apart: 7, of which 7 were waited for; matrix products, arithmetic and copies ran while one was open for 5% of the time, Pallas kernels for 0%

commit v1 on v0

--- a/solution.py
+++ b/solution.py
@@ -126,7 +126,11 @@
     def add_rows(weight_rows):
         return jnp.dot(features_all, weight_rows, preferred_element_type=jnp.float32)
 
-    query_sum = add_rows(lax.all_gather(w_query, "dp", axis=0, tiled=True))
+    query_sum = add_rows(
+        jnp.concatenate(
+            lax.all_to_all(jnp.stack([w_query] * lax.axis_size("dp")), "dp", 0, 0), axis=0
+        )
+    )
     key_sum = add_rows(lax.all_gather(w_key, "dp", axis=0, tiled=True))
     value_sum = add_rows(lax.all_gather(w_value, "dp", axis=0, tiled=True))
     context = attend(

time: 603 us -> 510 us (0.85)
  waiting for transfers between devices: 501 us -> 393 us
  starting transfers between devices: 35.6 us -> 47.2 us
    all_gather x1 -> x0, waiting for transfers between devices: 138 us -> none  [local(): query_sum = add_rows(lax.all_gather(w_query, 'dp', axis=0, tiled=True))]
    all_gather x1, waiting for transfers between devices: 147 us -> 187 us  [local(): value_sum = add_rows(lax.all_gather(w_value, 'dp', axis=0, tiled=True))]
    all_to_all x0 -> x1, starting transfers between devices: none -> 11.6 us  [local(): lax.all_to_all(jnp.stack([w_query] * lax.axis_size('dp')), 'dp', 0, 0)]
    all_gather x1, waiting for transfers between devices: 11.5 us -> 0.01 us  [local(): features_all = lax.all_gather(normed, 'mp', axis=1, tiled=True)]
  transfers between devices with their start and end apart: 7 -> 7, of which waited for: 7 -> 5; matrix products, arithmetic and copies ran while one was open for 5% -> 6% of each run, Pallas kernels for 0% -> 0%
where the time goes in v1:
time: 510 us; the launch traced here: 509 us
  waiting for transfers between devices  393 us (77%)
  starting transfers between devices  47.2 us (9%)
  local copies, waits for them, and re-layouts  20.3 us (4%)
  other arithmetic  15.6 us (3%)
  between operations  14.6 us (3%)
  matrix products  9.47 us (2%)
  blocking collectives  8.72 us (2%)
    all_gather x1, waiting for transfers between devices, local(): value_sum = add_rows(lax.all_gather(w_value, 'dp', axis=0, tiled=True))  187 us
    all_gather x1, waiting for transfers between devices, local(): key_sum = add_rows(lax.all_gather(w_key, 'dp', axis=0, tiled=True))  140 us
    all_to_all x1, waiting for transfers between devices, answer(): lax.all_to_all(joined_rows, 'dp', split_axis=0, concat_axis=0, tiled=True)  30.2 us
    all_to_all x1, waiting for transfers between devices, local(): lax.all_to_all(grad_buffer, 'dp', split_axis=0, concat_axis=0, tiled=True)  22.5 us
    all_to_all x1, starting transfers between devices, local(): lax.all_to_all(requests, 'dp', split_axis=0, concat_axis=0, tiled=True)  20.4 us
    all_to_all x1, waiting for transfers between devices, local(): lax.all_to_all(requests, 'dp', split_axis=0, concat_axis=0, tiled=True)  12.1 us
    all_to_all x1, starting transfers between devices, local(): lax.all_to_all(jnp.stack([w_query] * lax.axis_size('dp')), 'dp', 0, 0)  11.6 us
  transfers between devices with their start and end apart: 7, of which 5 were waited for; matrix products, arithmetic and copies ran while one was open for 6% of the time, Pallas kernels for 0%

profile of v1, /device:TPU:1, one launch (start us, length us, event | category | flops | bytes accessed | tf_op | source)
XLA Modules:
  0.0 509.1 jit_solution(3765466944165506280)
XLA Ops:
  7.2 0.0 copy-start
  7.2 0.8 fusion.22
  8.0 0.2 reduce_window_sum.11
  8.2 0.8 select_reduce_fusion
  9.0 0.7 fusion.24
  9.7 1.1 scatter_custom_fusion
  10.8 0.8 all_to_all.16
  11.5 20.4 %all-to-all-start = ((s32[128,1,2]{2,1,0:T(1,128)}), s32[128,1,2]{2,1,0:T(1,128)S(1)}, u32[]{:S(2)}, u32[]{:S(2)}) async-start(s32[128,1,2]{2,1,0:T(1,128)} %bitcast.4), calls=%async_computation | async-start | bytes 131072 | tf_op jit(solution)/shard_map/all_to_all | solution.py:105
  31.9 1.7 scatter_custom_fusion.1
  33.7 0.0 copy-start.2
  33.7 1.0 reshape.145
  34.7 12.1 %all-to-all-done = s32[128,1,2]{2,1,0:T(1,128)S(1)} async-done(((s32[128,1,2]{2,1,0:T(1,128)}), s32[128,1,2]{2,1,0:T(1,128)S(1)}, u32[]{:S(2)}, u32[]{:S(2)}) %all-to-all-start) | async-done | bytes 1056 | tf_op jit(solution)/shard_map/all_to_all | solution.py:105
  46.8 5.7 %all-to-all-start.3 = ((bf16[128,2,1024]{2,1,0:T(2,128)(2,1)}), bf16[128,2,1024]{2,1,0:T(2,128)(2,1)S(1)}, u32[]{:S(2)}, u32[]{:S(2)}) async-start(bf16[128,2,1024]{2,1,0:T(2,128)(2,1)} %reshape.145), calls=%async_computation.3 | async-start | bytes 1048576 | tf_op jit(solution)/shard_map/all_to_all | solution.py:113
  52.4 0.7 convert_element_type.54
  53.1 0.2 maximum_reduce_fusion
  53.3 0.1 reshape.150
  53.5 0.0 copy-done
  53.5 1.2 gather_fusion
  54.7 0.0 copy-start.1
  54.7 1.6 reshape.220
  56.3 0.0 copy-done.2
  56.3 1.2 gather_fusion.1
  57.5 1.6 reshape.221
  59.1 0.0 copy-done.1
  59.1 1.9 gather_fusion.2
  61.0 0.0 copy-start.5
  61.1 0.1 reshape.165
  61.2 0.0 copy-start.4
  61.2 22.5 %all-to-all-done.3 = bf16[128,2,1024]{2,1,0:T(2,128)(2,1)S(1)} async-done(((bf16[128,2,1024]{2,1,0:T(2,128)(2,1)}), bf16[128,2,1024]{2,1,0:T(2,128)(2,1)S(1)}, u32[]{:S(2)}, u32[]{:S(2)}) %all-to-all-start.3) | async-done | bytes 524320 | tf_op jit(solution)/shard_map/all_to_all | solution.py:113
  83.7 3.1 convert_multiply_fusion
  86.9 9.2 %all-to-all-start.1 = ((bf16[128,2,1024]{2,1,0:T(2,128)(2,1)}), bf16[128,2,1024]{2,1,0:T(2,128)(2,1)}, u32[]{:S(2)}, u32[]{:S(2)}) async-start(bf16[128,2,1024]{2,1,0:T(2,128)(2,1)} %get-tuple-element.13), calls=%async_computation.1 | async-start | bytes 1048576 | tf_op jit(solution)/shard_map/all_to_all | solution.py:28
  96.1 0.2 all-gather.4.cloned.1.call-start
  96.3 0.0 copy-done.5
  96.4 30.2 %all-to-all-done.1 = bf16[128,2,1024]{2,1,0:T(2,128)(2,1)} async-done(((bf16[128,2,1024]{2,1,0:T(2,128)(2,1)}), bf16[128,2,1024]{2,1,0:T(2,128)(2,1)}, u32[]{:S(2)}, u32[]{:S(2)}) %all-to-all-start.1) | async-done | bytes 524320 | tf_op jit(solution)/shard_map/all_to_all | solution.py:28
  126.6 1.2 reshape.140
  127.8 0.9 gather_fusion.3
  128.7 0.1 fusion.8
  128.8 8.7 %psum.7 = f32[128]{0:T(128)S(1)} all-reduce(f32[128]{0:T(128)S(1)} %fusion.8), channel_id=1, replica_groups=mesh['dp'=128,'mp'=4] {'mp'}, use_global_device_ids=true, to_apply=%region_4.5 | all-reduce | flops 128 | bytes 1024 | tf_op jit(solution)/shard_map/psum | solution.py:119
  137.6 0.9 fusion.10
  138.4 0.0 all-gather.4.cloned.1.call-update
  138.4 0.0 all-gather.6.cloned.1.call-start
  138.5 0.7 all-gather.6.cloned.1.call-update
  139.2 0.0 copy-done.4
  139.2 2.5 stack.2
  141.7 11.6 %all-to-all-start.2 = ((bf16[128,32,512]{2,1,0:T(8,128)(2,1)}), bf16[128,32,512]{2,1,0:T(8,128)(2,1)}, u32[]{:S(2)}, u32[]{:S(2)}) async-start(bf16[128,32,512]{2,1,0:T(8,128)(2,1)} %stack.2), calls=%async_computation.2 | async-start | bytes 8388608 | tf_op jit(solution)/shard_map/all_to_all | solution.py:131
  153.3 0.0 all-gather.8.cloned.1.call-start
  153.3 0.7 all-gather.8.cloned.1.call-update
  154.7 0.1 fusion.23
  154.8 1.7 reshape.200
  156.5 0.7 reshape.208
  157.2 4.3 scatter_custom_fusion.2
  161.5 3.6 scatter_custom_fusion.3
  165.1 187.3 %all-gather.6.cloned.1.call-done = bf16[4096,512]{1,0:T(8,128)(2,1)} async-done(((bf16[32,512]{1,0:T(8,128)(2,1)}), bf16[4096,512]{1,0:T(8,128)(2,1)}) %all-gather.6.cloned.1.call-update) | async-done | bytes 4194320 | tf_op jit(solution)/shard_map/all_gather | solution.py:135
  352.4 3.2 convolution_convert_fusion.2
  355.6 0.1 copy.32
  355.8 139.7 %all-gather.8.cloned.1.call-done = bf16[4096,512]{1,0:T(8,128)(2,1)} async-done(((bf16[32,512]{1,0:T(8,128)(2,1)}), bf16[4096,512]{1,0:T(8,128)(2,1)}) %all-gather.8.cloned.1.call-update) | async-done | bytes 4194320 | tf_op jit(solution)/shard_map/all_gather | solution.py:134
  495.4 0.0 copy-done.3
  495.4 2.9 fusion.7
  498.3 0.0 all-to-all-done.2
  498.3 2.9 fusion.6
  501.3 0.2 fusion.2
  501.5 0.1 fusion.28
  501.6 0.2 fusion.5
  501.8 0.8 copy.30
  (7 shorter events, 0.0 us)
Async XLA Ops:
  7.2 46.3 %copy-start = (bf16[256,1024]{1,0:T(8,128)(2,1)S(1)}, bf16[256,1024]{1,0:T(8,128)(2,1)}, u32[]{:S(2)}) copy-start(bf16[256,1024]{1,0:T(8,128)(2,1)} %param.15) | copy-start | bytes 1572868
  11.5 35.2 %all-to-all-start = ((s32[128,1,2]{2,1,0:T(1,128)}), s32[128,1,2]{2,1,0:T(1,128)S(1)}, u32[]{:S(2)}, u32[]{:S(2)}) async-start(s32[128,1,2]{2,1,0:T(1,128)} %bitcast.4), calls=%async_computation | async-start | bytes 131072 | tf_op jit(solution)/shard_map/all_to_all | solution.py:105
  33.7 22.6 %copy-start.2 = (bf16[256,1024]{1,0:T(8,128)(2,1)S(1)}, bf16[256,1024]{1,0:T(8,128)(2,1)}, u32[]{:S(2)}) copy-start(bf16[256,1024]{1,0:T(8,128)(2,1)} %param.16) | copy-start | bytes 1572868
  46.8 37.0 %all-to-all-start.3 = ((bf16[128,2,1024]{2,1,0:T(2,128)(2,1)}), bf16[128,2,1024]{2,1,0:T(2,128)(2,1)S(1)}, u32[]{:S(2)}, u32[]{:S(2)}) async-start(bf16[128,2,1024]{2,1,0:T(2,128)(2,1)} %reshape.145), calls=%async_computation.3 | async-start | bytes 1048576 | tf_op jit(solution)/shard_map/all_to_all | solution.py:113
  54.7 4.4 copy-start.1
  61.0 35.3 %copy-start.5 = (bf16[1024]{0:T(1024)(128)(2,1)S(1)}, bf16[1024]{0:T(1024)(128)(2,1)}, u32[]{:S(2)}) copy-start(bf16[1024]{0:T(1024)(128)(2,1)} %param.19) | copy-start | bytes 6148
  61.2 78.0 %copy-start.4 = (bf16[32,512]{1,0:T(8,128)(2,1)S(1)}, bf16[32,512]{1,0:T(8,128)(2,1)}, u32[]{:S(2)}) copy-start(bf16[32,512]{1,0:T(8,128)(2,1)} %param.20) | copy-start | bytes 98308
  86.9 39.7 %all-to-all-start.1 = ((bf16[128,2,1024]{2,1,0:T(2,128)(2,1)}), bf16[128,2,1024]{2,1,0:T(2,128)(2,1)}, u32[]{:S(2)}, u32[]{:S(2)}) async-start(bf16[128,2,1024]{2,1,0:T(2,128)(2,1)} %get-tuple-element.13), calls=%async_computation.1 | async-start | bytes 1048576 | tf_op jit(solution)/shard_map/all_to_all | solution.py:28
  96.1 69.0 %all-gather.4.cloned.1.call-start = ((), (), s32[]{:S(2)}) async-start(), calls=%async_computation.4 | async-start | bytes 1310720 | tf_op jit(solution)/shard_map/all_gather | solution.py:124
  138.4 214.0 %all-gather.6.cloned.1.call-start = ((), (), s32[]{:S(2)}) async-start(), calls=%async_computation.5 | async-start | bytes 4227072 | tf_op jit(solution)/shard_map/all_gather | solution.py:135
  141.7 356.6 %all-to-all-start.2 = ((bf16[128,32,512]{2,1,0:T(8,128)(2,1)}), bf16[128,32,512]{2,1,0:T(8,128)(2,1)}, u32[]{:S(2)}, u32[]{:S(2)}) async-start(bf16[128,32,512]{2,1,0:T(8,128)(2,1)} %stack.2), calls=%async_computation.2 | async-start | bytes 8388608 | tf_op jit(solution)/shard_map/all_to_all | solution.py:131
  153.3 342.1 %all-gather.8.cloned.1.call-start = ((), (), s32[]{:S(2)}) async-start(), calls=%async_computation.6 | async-start | bytes 4227072 | tf_op jit(solution)/shard_map/all_gather | solution.py:134
  165.1 330.3 %copy-start.3 = (bf16[128,4096]{1,0:T(8,128)(2,1)S(1)}, bf16[128,4096]{1,0:T(8,128)(2,1)}, u32[]{:S(2)}) copy-start(bf16[128,4096]{1,0:T(8,128)(2,1)} %all-gather.4.cloned.1.call-done) | copy-start | bytes 3145732
Sparse Core Ops, SparseCore 0:
  138.6 24.4 all-gather.3
  166.2 186.1 all-gather.5
  355.5 139.8 all-gather.7
